TPU v7x, 256 devices: a whole 4x4x8 slice. The times are simulated.
256 devices in a mesh: dp: 8 (over x, core), cut: 32 (over y, z).
Axes of the slice: x: 4, y: 4, z: 8, core: 2. Of those that a mesh axis runs over, the one named last changes fastest.
Arguments:
- node_feat: bfloat16 [128, 262144], P(None, ('dp', 'cut')), parts along dimension 1, may hold values from -6 to 6
- edge_feat: bfloat16 [128, 1048576], P(None, ('dp', 'cut')), parts along dimension 1, may hold values from -6 to 6
- route: int32 [256, 32, 128], P(('dp', 'cut')), parts along dimension 0, may hold values from 0 to 1023, as said below
- block_tile: int32 [8192, 2], P(('dp', 'cut')), parts along dimension 0, may hold values from 0 to 39
- block_offset: int32 [8192, 2, 128], P(('dp', 'cut')), parts along dimension 0, may hold values from 0 to 127
- block_count: int32 [8192], P(('dp', 'cut')), parts along dimension 0, may hold values from 1 to 128, as said below
- w_edge1: bfloat16 [128, 384], replicated, may hold values from -0.3125 to 0.3125
- bias_edge1: float32 [128], replicated, may hold values from -3 to 3
- w_edge2: bfloat16 [128, 128], replicated, may hold values from -0.5 to 0.5
- gain_edge: float32 [128], replicated, may hold values from 0.1 to 1.9
- shift_edge: float32 [128], replicated, may hold values from -3 to 3
- w_node1: bfloat16 [128, 256], replicated, may hold values from -0.375 to 0.375
- bias_node1: float32 [128], replicated, may hold values from -3 to 3
- w_node2: bfloat16 [128, 128], replicated, may hold values from -0.5 to 0.5
- gain_node: float32 [128], replicated, may hold values from 0.1 to 1.9
- shift_node: float32 [128], replicated, may hold values from -3 to 3
- node_cot: bfloat16 [128, 262144], P(None, ('dp', 'cut')), parts along dimension 1, may hold values from -6 to 6
Outputs:
- node_out: bfloat16 [128, 262144], P(None, ('dp', 'cut')), parts along dimension 1
- node_grad: float32 [128, 262144], P(None, ('dp', 'cut')), parts along dimension 1
- edge_grad: bfloat16 [128, 1048576], P(None, ('dp', 'cut')), parts along dimension 1
- param_grad: float32 [923648], P('dp'), parts along dimension 0
There are 8 independent parts, one for each index of `dp`. A program takes and returns all parts, laid end to end along the dimension named above; an argument that names none is the same for every part. Nothing has to cross between parts.
Inputs may be any that keep to these rules, and one draw needn't show every extreme that they name: route[c, p, :] holds 128 distinct master rows of partition p. `block_count`: the first block of each partition is full.
All inputs are finite; a program needn't handle non-finite values.
Results may differ from a plain program's by a relative error of at most 0.024.
Values may be sent and summed in bfloat16 or wider, within the bound.
No kernel may reach another device: no remote copies, remote signals or barrier semaphores. Data moves between devices by JAX's collectives and lax.ppermute only.
A program may use at most 128 MiB of HBM per device.

v0:
```python
import math
import jax
import jax.numpy as jnp
from jax import lax
from jax.sharding import PartitionSpec as P


def silu_slope(values):
    sigmoid_val = jax.nn.sigmoid(values)
    return sigmoid_val * (1.0 + values * (1.0 - sigmoid_val))


def layer_norm(values):
    centred = values - jnp.mean(values, axis=0, keepdims=True)
    inverse = lax.rsqrt(jnp.mean(centred * centred, axis=0, keepdims=True) + 1e-05)
    return (centred * inverse, inverse)


def norm_back(upstream, normed, inverse, gain_vec):
    scaled = upstream * gain_vec[:, None]
    return inverse * (
        scaled
        - jnp.mean(scaled, axis=0, keepdims=True)
        - normed * jnp.mean(scaled * normed, axis=0, keepdims=True)
    )


def row_contract(left, right):
    return lax.dot_general(
        left, right, (((1,), (1,)), ((), ())), preferred_element_type=jnp.float32
    )


def lead_contract(weight, values):
    return lax.dot_general(
        weight, values, (((0,), (0,)), ((), ())), preferred_element_type=jnp.float32
    )


def per_device(
    node_feat,
    edge_feat,
    route,
    block_tile,
    block_offset,
    block_count,
    w_edge1,
    bias_edge1,
    w_edge2,
    gain_edge,
    shift_edge,
    w_node1,
    bias_node1,
    w_node2,
    gain_node,
    shift_node,
    node_cot,
):
    latent = node_feat.shape[0]
    masters = node_feat.shape[1]
    peer_count = lax.axis_size("cut")
    total_nodes = masters * peer_count
    total_edges = edge_feat.shape[1] * peer_count
    mirror_index = lax.all_to_all(route[0], "cut", split_axis=0, concat_axis=0, tiled=True).reshape(
        -1
    )

    def fetch_mirrors(master_part):
        outgoing = jnp.take(master_part, mirror_index, axis=1)
        result = lax.all_to_all(outgoing, "cut", split_axis=1, concat_axis=1, tiled=True)
        return result

    def reduce_mirrors(master_part, mirror_part):
        returned = lax.all_to_all(
            mirror_part.astype(jnp.bfloat16), "cut", split_axis=1, concat_axis=1, tiled=True
        ).astype(mirror_part.dtype)
        result = master_part.at[:, mirror_index].add(returned)
        return result

    columns = 128 * block_tile[:, :, None] + block_offset
    send_cols = columns[:, 0, :].reshape(-1)
    recv_cols = columns[:, 1, :].reshape(-1)
    live_mask = (
        (jnp.arange(block_offset.shape[2], dtype=jnp.int32)[None, :] < block_count[:, None])
        .reshape(-1)
        .astype(jnp.float32)
    )
    node_table = jnp.concatenate([node_feat, fetch_mirrors(node_feat)], axis=1)
    local_width = node_table.shape[1]
    stacked = jnp.concatenate(
        [
            edge_feat,
            jnp.take(node_table, send_cols, axis=1),
            jnp.take(node_table, recv_cols, axis=1),
        ],
        axis=0,
    )
    edge_pre = jnp.dot(w_edge1, stacked, preferred_element_type=jnp.float32) + bias_edge1[:, None]
    edge_hidden = jax.nn.silu(edge_pre).astype(jnp.bfloat16)
    edge_post = jnp.dot(w_edge2, edge_hidden, preferred_element_type=jnp.float32)
    edge_normed, edge_inv = layer_norm(edge_post)
    message = (gain_edge[:, None] * edge_normed + shift_edge[:, None]) * live_mask[None, :]
    local_sums = jnp.zeros((latent, local_width), jnp.float32).at[:, recv_cols].add(message)
    aggregate = reduce_mirrors(local_sums[:, :masters], local_sums[:, masters:])
    agg_low = aggregate.astype(jnp.bfloat16)
    node_input = jnp.concatenate([node_feat, agg_low], axis=0)
    node_pre = (
        jnp.dot(w_node1, node_input, preferred_element_type=jnp.float32) + bias_node1[:, None]
    )
    node_hidden = jax.nn.silu(node_pre).astype(jnp.bfloat16)
    node_post = jnp.dot(w_node2, node_hidden, preferred_element_type=jnp.float32)
    node_normed, node_inv = layer_norm(node_post)
    node_out = (
        node_feat.astype(jnp.float32) + gain_node[:, None] * node_normed + shift_node[:, None]
    ).astype(jnp.bfloat16)
    upstream = node_cot.astype(jnp.float32)
    grad_gain_node = jnp.sum(upstream * node_normed, axis=1)
    grad_shift_node = jnp.sum(upstream, axis=1)
    grad_node_post = norm_back(upstream, node_normed, node_inv, gain_node).astype(jnp.bfloat16)
    grad_w_node2 = row_contract(grad_node_post, node_hidden)
    grad_node_full = lead_contract(w_node2, grad_node_post) * silu_slope(node_pre)
    grad_node_pre = grad_node_full.astype(jnp.bfloat16)
    grad_w_node1 = row_contract(grad_node_pre, node_input)
    grad_bias_node1 = jnp.sum(grad_node_full, axis=1)
    node_direct = lead_contract(w_node1[:, :latent], grad_node_pre)
    grad_agg = lead_contract(w_node1[:, latent:], grad_node_pre).astype(jnp.bfloat16)
    node_vec = jnp.concatenate(
        [
            grad_w_node1.reshape(-1),
            grad_bias_node1,
            grad_w_node2.reshape(-1),
            grad_gain_node,
            grad_shift_node,
        ]
    )
    agg_table = jnp.concatenate([grad_agg, fetch_mirrors(grad_agg)], axis=1)
    grad_message = jnp.take(agg_table, recv_cols, axis=1).astype(jnp.float32) * live_mask[None, :]
    grad_gain_edge = jnp.sum(grad_message * edge_normed, axis=1)
    grad_shift_edge = jnp.sum(grad_message, axis=1)
    grad_edge_post = norm_back(grad_message, edge_normed, edge_inv, gain_edge).astype(jnp.bfloat16)
    grad_w_edge2 = row_contract(grad_edge_post, edge_hidden)
    grad_edge_full = lead_contract(w_edge2, grad_edge_post) * silu_slope(edge_pre)
    grad_edge_pre = grad_edge_full.astype(jnp.bfloat16)
    grad_w_edge1 = row_contract(grad_edge_pre, stacked)
    grad_bias_edge1 = jnp.sum(grad_edge_full, axis=1)
    edge_grad = lead_contract(w_edge1[:, :latent], grad_edge_pre).astype(jnp.bfloat16)
    grad_send = lead_contract(w_edge1[:, latent : 2 * latent], grad_edge_pre)
    grad_recv = lead_contract(w_edge1[:, 2 * latent :], grad_edge_pre)
    grad_table = (
        jnp.zeros((latent, local_width), jnp.float32)
        .at[:, send_cols]
        .add(grad_send)
        .at[:, recv_cols]
        .add(grad_recv)
    )
    node_grad = (
        upstream + node_direct + reduce_mirrors(grad_table[:, :masters], grad_table[:, masters:])
    )
    edge_vec = jnp.concatenate(
        [
            grad_w_edge1.reshape(-1),
            grad_bias_edge1,
            grad_w_edge2.reshape(-1),
            grad_gain_edge,
            grad_shift_edge,
        ]
    )
    summed = lax.psum(jnp.concatenate([edge_vec, node_vec]).astype(jnp.bfloat16), "cut").astype(
        jnp.float32
    )
    edge_summed = summed[: edge_vec.shape[0]]
    node_summed = summed[edge_vec.shape[0] :]
    param_grad = jnp.concatenate(
        [edge_summed / math.sqrt(total_edges), node_summed / math.sqrt(total_nodes)]
    )
    return (node_out, node_grad, edge_grad, param_grad)


def solution(mesh):
    in_specs = (
        P(None, ("dp", "cut")),
        P(None, ("dp", "cut")),
        P(("dp", "cut"), None, None),
        P(("dp", "cut"), None),
        P(("dp", "cut"), None, None),
        P(("dp", "cut")),
        P(),
        P(),
        P(),
        P(),
        P(),
        P(),
        P(),
        P(),
        P(),
        P(),
        P(None, ("dp", "cut")),
    )
    out_specs = (P(None, ("dp", "cut")), P(None, ("dp", "cut")), P(None, ("dp", "cut")), P("dp"))
    return jax.shard_map(
        per_device, mesh=mesh, in_specs=in_specs, out_specs=out_specs, check_vma=False
    )
```

profile of v0, /device:TPU:2, one launch (start us, length us, event | category | flops | bytes accessed | tf_op | source)
XLA Modules:
  0.0 506.6 jit_solution(10482661762203878273)
XLA Ops:
  7.2 11.5 %all-to-all-start = ((s32[32,1,128]{2,1,0:T(1,128)}), s32[32,1,128]{2,1,0:T(1,128)S(1)}, u32[]{:S(2)}, u32[]{:S(2)}) async-start(s32[32,1,128]{2,1,0:T(1,128)} %bitcast.144), calls=%async_computation | async-start | bytes 32768 | tf_op jit(solution)/shard_map/all_to_all | solution.py:64
  19.5 0.9 broadcast_add_fusion
  20.3 1.1 copy.38
  21.4 7.0 %all-to-all-done = s32[32,1,128]{2,1,0:T(1,128)S(1)} async-done(((s32[32,1,128]{2,1,0:T(1,128)}), s32[32,1,128]{2,1,0:T(1,128)S(1)}, u32[]{:S(2)}, u32[]{:S(2)}) %all-to-all-start) | async-done | bytes 16416 | tf_op jit(solution)/shard_map/all_to_all | solution.py:64
  28.4 12.1 %gather_fusion = bf16[4096,128]{1,0:T(8,128)(2,1)S(1)} fusion(bf16[128,1024]{0,1:T(8,128)(2,1)S(1)} %copy.38, s32[4096]{0:T(1024)S(1)} %fusion.48), kind=kCustom, calls=%fused_computation.clone | custom fusion | bytes 2113536 | tf_op jit(solution)/shard_map/jit(_take)/gather | solution.py:69
  40.6 2.9 broadcast_select_fusion.1
  43.5 3.9 all-to-all-start.1
  47.5 1.3 copy.36
  49.6 25.4 %all-to-all-done.1 = bf16[128,32,128]{0,2,1:T(8,128)(2,1)S(1)} async-done(((bf16[128,32,128]{0,2,1:T(8,128)(2,1)}), bf16[128,32,128]{0,2,1:T(8,128)(2,1)S(1)}, u32[]{:S(2)}, u32[]{:S(2)}) %all-to-all-start.1) | async-done | bytes 1048608 | tf_op jit(solution)/shard_map/all_to_all | solution.py:70
  75.1 12.1 %gather_fusion.1 = bf16[4096,128]{1,0:T(8,128)(2,1)S(1)} fusion(bf16[128,5120]{0,1:T(8,128)(2,1)S(1)} %pad_maximum_fusion.1, s32[4096]{0:T(1024)S(1)} %fusion.49), kind=kCustom, calls=%fused_computation.1.clone | custom fusion | bytes 2113536 | tf_op jit(solution)/shard_map/jit(_take)/gather | solution.py:93
  87.2 15.0 %gather_fusion.2 = bf16[4096,128]{1,0:T(8,128)(2,1)} fusion(bf16[128,5120]{0,1:T(8,128)(2,1)S(1)} %pad_maximum_fusion.1, s32[4096]{0:T(1024)S(1)} %fusion.50), kind=kCustom, calls=%fused_computation.3.clone | custom fusion | bytes 2113536 | tf_op jit(solution)/shard_map/jit(_take)/gather | solution.py:94
  102.3 3.1 select_bitcast_fusion
  105.4 2.3 multiply_convert_fusion
  109.9 1.8 copy.37
  111.8 23.3 %scatter_custom_fusion = f32[128,5120]{0,1:T(8,128)S(1)} fusion(s32[4096]{0:T(1024)S(1)} %bitcast.142, f32[4096,128]{1,0:T(8,128)} %copy.37, f32[]{:T(128)} %constant.26.clone.1), kind=kCustom, calls=%fused_computation.47 | custom fusion | flops 524288 | bytes 2621952 | tf_op jit(solution)/shard_map/scatter-add | solution.py:103
  135.1 1.1 slice.89
  136.2 5.1 %all-to-all-start.2 = ((bf16[128,32,128]{0,2,1:T(8,128)(2,1)}), bf16[128,32,128]{0,2,1:T(8,128)(2,1)}, u32[]{:S(2)}, u32[]{:S(2)}) async-start(bf16[128,32,128]{0,2,1:T(8,128)(2,1)} %bitcast.134), calls=%async_computation.2 | async-start | bytes 2097152 | tf_op jit(solution)/shard_map/all_to_all | solution.py:74
  141.4 27.5 %all-to-all-done.2 = bf16[128,32,128]{0,2,1:T(8,128)(2,1)} async-done(((bf16[128,32,128]{0,2,1:T(8,128)(2,1)}), bf16[128,32,128]{0,2,1:T(8,128)(2,1)}, u32[]{:S(2)}, u32[]{:S(2)}) %all-to-all-start.2) | async-done | bytes 1048608 | tf_op jit(solution)/shard_map/all_to_all | solution.py:74
  168.9 23.1 %scatter_custom_fusion.1 = f32[128,1024]{0,1:T(8,128)S(1)} fusion(f32[128,1024]{0,1:T(8,128)S(1)} %slice.66, s32[4096]{0:T(1024)S(1)} %bitcast.145, bf16[128,4096]{0,1:T(8,128)(2,1)} %bitcast.39), kind=kCustom, calls=%fused_computation.22 | custom fusion | flops 1048576 | bytes 1572864 | tf_op jit(solution)/shard_map/scatter-add | solution.py:77
  192.2 1.2 multiply_convert_fusion.1
  194.6 1.0 fusion.35
  195.6 0.9 fusion.62
  196.7 12.1 %gather_fusion.3 = bf16[4096,128]{1,0:T(8,128)(2,1)S(1)} fusion(bf16[128,1024]{0,1:T(8,128)(2,1)S(1)} %fusion.25, s32[4096]{0:T(1024)S(1)} %fusion.48), kind=kCustom, calls=%fused_computation.2.clone | custom fusion | bytes 2113536 | tf_op jit(solution)/shard_map/jit(_take)/gather | solution.py:69
  208.8 2.9 broadcast_select_fusion
  211.7 5.0 all-to-all-start.3
  217.8 0.8 fusion.29
  218.6 25.7 %all-to-all-done.3 = bf16[128,32,128]{0,2,1:T(8,128)(2,1)S(1)} async-done(((bf16[128,32,128]{0,2,1:T(8,128)(2,1)}), bf16[128,32,128]{0,2,1:T(8,128)(2,1)S(1)}, u32[]{:S(2)}, u32[]{:S(2)}) %all-to-all-start.3) | async-done | bytes 1048608 | tf_op jit(solution)/shard_map/all_to_all | solution.py:70
  244.4 15.0 %gather_fusion.4 = bf16[4096,128]{1,0:T(8,128)(2,1)} fusion(bf16[128,5120]{0,1:T(8,128)(2,1)S(1)} %pad_maximum_fusion.2, s32[4096]{0:T(1024)S(1)} %copy-done.18), kind=kCustom, calls=%fused_computation.4.clone | custom fusion | bytes 2113536 | tf_op jit(solution)/shard_map/jit(_take)/gather | solution.py:137
  259.5 1.6 copy.40
  261.4 2.5 fusion.12
  265.5 1.2 copy-done.41
  266.7 1.5 fusion.58
  268.5 1.4 fusion.26
  269.9 1.4 fusion.2
  271.3 1.8 fusion.42
  273.1 1.7 fusion.44
  274.8 23.3 %scatter_custom_fusion.2 = f32[128,5120]{0,1:T(8,128)S(1)} fusion(s32[4096]{0:T(1024)} %bitcast.147, f32[4096,128]{1,0:T(8,128)} %fusion.44, f32[]{:T(128)} %constant.26.clone.1), kind=kCustom, calls=%fused_computation.45 | custom fusion | flops 524288 | bytes 2621952 | tf_op jit(solution)/shard_map/scatter-add | solution.py:152
  298.1 23.8 %scatter_fusion = f32[128,5120]{0,1:T(8,128)S(1)} fusion(f32[128,5120]{0,1:T(8,128)S(1)} %scatter_custom_fusion.2, s32[4096]{0:T(1024)S(1)} %bitcast.143, f32[4096,128]{1,0:T(8,128)} %fusion.42), kind=kCustom, calls=%fused_computation.8 | custom fusion | flops 524288 | bytes 6307840 | tf_op jit(solution)/shard_map/scatter-add | solution.py:154
  322.0 1.1 slice.88
  323.1 1.0 reshape.207
  326.8 0.8 dynamic-update-slice.6
  327.6 1.1 dynamic-update-slice.7
  329.9 2.3 copy.44
  332.8 5.0 all-to-all-start.4
  337.8 136.4 %all-reduce.2.cloned.1.call-done = bf16[115456]{0:T(1024)(128)(2,1)} async-done(((bf16[115456]{0:T(1024)(128)(2,1)}), bf16[115456]{0:T(1024)(128)(2,1)}) %all-reduce.2.cloned.1.call-update) | async-done | bytes 230928 | tf_op jit(solution)/shard_map/psum | solution.py:168
  474.2 1.0 convert_element_type.94
  476.1 22.7 %scatter_custom_fusion.4 = f32[128,1024]{0,1:T(8,128)S(1)} fusion(f32[128,1024]{0,1:T(8,128)S(1)} %copy.42, s32[4096]{0:T(1024)} %bitcast.146, bf16[128,4096]{0,1:T(8,128)(2,1)S(1)} %bitcast.132), kind=kCustom, calls=%fused_computation.20 | custom fusion | flops 1048576 | bytes 1572864 | tf_op jit(solution)/shard_map/scatter-add | solution.py:77
  498.8 1.0 copy.43
  (137 shorter events, 14.1 us)
Async XLA Ops:
  7.2 100.6 %copy-start = (bf16[128,128]{1,0:T(8,128)(2,1)S(1)}, bf16[128,128]{1,0:T(8,128)(2,1)}, u32[]{:S(2)}) copy-start(bf16[128,128]{1,0:T(8,128)(2,1)} %param.29) | copy-start | bytes 98308
  7.2 21.2 %all-to-all-start = ((s32[32,1,128]{2,1,0:T(1,128)}), s32[32,1,128]{2,1,0:T(1,128)S(1)}, u32[]{:S(2)}, u32[]{:S(2)}) async-start(s32[32,1,128]{2,1,0:T(1,128)} %bitcast.144), calls=%async_computation | async-start | bytes 32768 | tf_op jit(solution)/shard_map/all_to_all | solution.py:64
  40.6 6.8 %copy-start.38 = (s32[32]{0:T(128)S(1)}, s32[32]{0:T(128)}, u32[]{:S(2)}) copy-start(s32[32]{0:T(128)} %param.26) | copy-start | bytes 388
  40.6 6.9 %copy-start.8 = (bf16[128,4096]{1,0:T(8,128)(2,1)S(1)}, bf16[128,4096]{1,0:T(8,128)(2,1)}, u32[]{:S(2)}) copy-start(bf16[128,4096]{1,0:T(8,128)(2,1)} %param.22) | copy-start | bytes 3145732
  43.5 31.5 %all-to-all-start.1 = ((bf16[128,32,128]{0,2,1:T(8,128)(2,1)}), bf16[128,32,128]{0,2,1:T(8,128)(2,1)S(1)}, u32[]{:S(2)}, u32[]{:S(2)}) async-start(bf16[128,32,128]{0,2,1:T(8,128)(2,1)} %bitcast.6), calls=%async_computation.1 | async-start | bytes 2097152 | tf_op jit(solution)/shard_map/all_to_all | solution.py:70
  48.9 53.4 %copy-start.25 = (pred[4096]{0:T(1024)(128)(4,1)}, pred[4096]{0:T(1024)(128)(4,1)S(1)}, u32[]{:S(2)}) copy-start(pred[4096]{0:T(1024)(128)(4,1)S(1)} %compare_and_fusion) | copy-start | bytes 12292
  48.9 38.3 %copy-start.17 = (s32[4096]{0:T(1024)}, s32[4096]{0:T(1024)S(1)}, u32[]{:S(2)}) copy-start(s32[4096]{0:T(1024)S(1)} %fusion.50) | copy-start | bytes 49156
  49.6 62.2 %copy-start.21 = (s32[4096,1]{0,1:T(1,128)}, s32[4096,1]{0,1:T(1,128)S(1)}, u32[]{:S(2)}) copy-start(s32[4096,1]{0,1:T(1,128)S(1)} %get-tuple-element.26) | copy-start | bytes 49156
  102.3 3.1 copy-start.9
  102.3 3.1 copy-start.19
  102.3 3.1 copy-start.39
  105.4 2.4 copy-start.12
  105.4 2.3 copy-start.14
  107.7 1.0 copy-start.3
  107.7 1.8 copy-start.29
  107.7 1.8 copy-start.36
  108.2 1.3 copy-start.1
  136.2 32.8 %all-to-all-start.2 = ((bf16[128,32,128]{0,2,1:T(8,128)(2,1)}), bf16[128,32,128]{0,2,1:T(8,128)(2,1)}, u32[]{:S(2)}, u32[]{:S(2)}) async-start(bf16[128,32,128]{0,2,1:T(8,128)(2,1)} %bitcast.134), calls=%async_computation.2 | async-start | bytes 2097152 | tf_op jit(solution)/shard_map/all_to_all | solution.py:74
  141.3 50.8 %copy-start.40 = (f32[128]{0:T(128)S(1)}, f32[128]{0:T(128)}, u32[]{:S(2)}) copy-start(f32[128]{0:T(128)} %param.33) | copy-start | bytes 1540
  141.4 52.1 %copy-start.28 = (s32[4096,1]{0,1:T(1,128)}, s32[4096,1]{0,1:T(1,128)S(1)}, u32[]{:S(2)}) copy-start(s32[4096,1]{0,1:T(1,128)S(1)} %compare_select_fusion.1) | copy-start | bytes 49156
  192.1 1.3 copy-start.27
  192.1 1.6 copy-start.5
  192.2 1.6 copy-start.31
  192.2 2.4 copy-start.11
  192.2 2.4 copy-start.37
  194.6 1.9 copy-start.23
  196.5 21.0 %copy-start.6 = (bf16[128,1024]{0,1:T(8,128)(2,1)}, bf16[128,1024]{0,1:T(8,128)(2,1)S(1)}, u32[]{:S(2)}) copy-start(bf16[128,1024]{0,1:T(8,128)(2,1)S(1)} %get-tuple-element.39) | copy-start | bytes 786436
  211.7 32.6 %all-to-all-start.3 = ((bf16[128,32,128]{0,2,1:T(8,128)(2,1)}), bf16[128,32,128]{0,2,1:T(8,128)(2,1)S(1)}, u32[]{:S(2)}, u32[]{:S(2)}) async-start(bf16[128,32,128]{0,2,1:T(8,128)(2,1)} %bitcast.28), calls=%async_computation.3 | async-start | bytes 2097152 | tf_op jit(solution)/shard_map/all_to_all | solution.py:70
  216.7 257.5 %all-reduce.2.cloned.1.call-start = ((), (), s32[]{:S(2)}) async-start(), calls=%async_computation.5 | async-start | bytes 462848 | tf_op jit(solution)/shard_map/psum | solution.py:168
  217.4 27.0 %copy-start.18 = (s32[4096]{0:T(1024)S(1)}, s32[4096]{0:T(1024)}, u32[]{:S(2)}) copy-start(s32[4096]{0:T(1024)} %copy-done.17) | copy-start | bytes 49156
  259.5 1.9 copy-start.2
  261.4 2.5 copy-start.26
  261.4 2.5 copy-start.30
  263.8 1.2 copy-start.4
  265.1 1.6 copy-start.41
  266.7 1.5 copy-start.10
  266.7 1.5 copy-start.13
  266.7 1.9 copy-start.15
  268.5 1.4 copy-start.20
  274.8 23.3 %copy-start.22 = (s32[4096,1]{0,1:T(1,128)S(1)}, s32[4096,1]{0,1:T(1,128)}, u32[]{:S(2)}) copy-start(s32[4096,1]{0,1:T(1,128)} %copy-done.21) | copy-start | bytes 49156
  322.0 3.5 copy-start.35
  322.0 3.8 copy-start.34
  322.0 6.7 %copy-start.32 = (bf16[128]{0:T(256)(128)(2,1)S(1)}, bf16[128]{0:T(256)(128)(2,1)}, u32[]{:S(2)}) copy-start(bf16[128]{0:T(256)(128)(2,1)} %get-tuple-element.18) | copy-start | bytes 772
  322.0 7.0 %copy-start.33 = (bf16[128]{0:T(256)(128)(2,1)S(1)}, bf16[128]{0:T(256)(128)(2,1)}, u32[]{:S(2)}) copy-start(bf16[128]{0:T(256)(128)(2,1)} %reduce.4) | copy-start | bytes 772
  323.1 9.2 %copy-start.7 = (bf16[128,1024]{0,1:T(8,128)(2,1)S(1)}, bf16[128,1024]{0,1:T(8,128)(2,1)}, u32[]{:S(2)}) copy-start(bf16[128,1024]{0,1:T(8,128)(2,1)} %copy-done.6) | copy-start | bytes 786436
  323.1 9.2 %copy-start.24 = (bf16[128,256]{1,0:T(8,128)(2,1)S(1)}, bf16[128,256]{1,0:T(8,128)(2,1)}, u32[]{:S(2)}) copy-start(bf16[128,256]{1,0:T(8,128)(2,1)} %param.32) | copy-start | bytes 196612
  329.1 0.7 copy-start.16
  332.8 143.2 %all-to-all-start.4 = ((bf16[128,32,128]{0,2,1:T(8,128)(2,1)}), bf16[128,32,128]{0,2,1:T(8,128)(2,1)S(1)}, u32[]{:S(2)}, u32[]{:S(2)}) async-start(bf16[128,32,128]{0,2,1:T(8,128)(2,1)} %bitcast.32), calls=%async_computation.4 | async-start | bytes 2097152 | tf_op jit(solution)/shard_map/all_to_all | solution.py:74
Sparse Core Ops, SparseCore 0:
  330.0 144.1 all-reduce.1
where the time goes:
time: 508 us; the launch traced here: 507 us
  waiting for transfers between devices  222 us (44%)
  other arithmetic  136 us (27%)
  local copies, waits for them, and re-layouts  88.5 us (17%)
  starting transfers between devices  30.5 us (6%)
  matrix products  14.8 us (3%)
  between operations  14.8 us (3%)
    psum x1, waiting for transfers between devices, per_device(): lax.psum(jnp.concatenate([edge_vec, node_vec]).astype(jnp.bfloat16), 'cut')  136 us
    all_to_all x2, waiting for transfers between devices, fetch_mirrors(): lax.all_to_all(outgoing, 'cut', split_axis=1, concat_axis=1, tiled=True)  51.1 us
    scatter-add x2, other arithmetic, per_device(): grad_table = jnp.zeros((latent, local_width), jnp.float32).at[:, send_col...  47.1 us
    scatter-add x2, other arithmetic, reduce_mirrors(): result = master_part.at[:, mirror_index].add(returned)  45.9 us
    all_to_all x2, waiting for transfers between devices, reduce_mirrors(): lax.all_to_all(mirror_part.astype(jnp.bfloat16), 'cut', split_axis=1, con...  27.5 us
    gather x2, local copies, waits for them, and re-layouts, fetch_mirrors(): outgoing = jnp.take(master_part, mirror_index, axis=1)  24.3 us
    scatter-add x1, other arithmetic, per_device(): jnp.zeros((latent, local_width), jnp.float32).at[:, recv_cols].add(message)  23.3 us
    gather x2, local copies, waits for them, and re-layouts, per_device(): jnp.take(agg_table, recv_cols, axis=1).astype(jnp.float32)  16.7 us
  transfers between devices with their start and end apart: 6, of which 5 were waited for; matrix products, arithmetic and copies ran while one was open for 2% of the time, Pallas kernels for 0%

commit v1 on v0

--- a/solution.py
+++ b/solution.py
@@ -1,8 +1,23 @@
+import functools
 import math
 import jax
 import jax.numpy as jnp
 from jax import lax
 from jax.sharding import PartitionSpec as P
+
+
+def expand_the_racks(inp, a_name):
+    a_next = lax.axis_size(a_name)
+    v_now = jnp.concatenate(
+        lax.all_to_all(
+            jnp.stack(jnp.split(inp, a_next, 1), 0), axis_name=a_name, split_axis=0, concat_axis=0
+        ),
+        1,
+    )
+    return v_now
+
+
+enter_the_figure = functools.partial(expand_the_racks, a_name="cut")
 
 
 def silu_slope(values):
@@ -67,7 +82,7 @@
 
     def fetch_mirrors(master_part):
         outgoing = jnp.take(master_part, mirror_index, axis=1)
-        result = lax.all_to_all(outgoing, "cut", split_axis=1, concat_axis=1, tiled=True)
+        result = enter_the_figure(outgoing)
         return result
 
     def reduce_mirrors(master_part, mirror_part):

time: 508 us -> 546 us (1.075)
  local copies, waits for them, and re-layouts: 88.5 us -> 128 us
    unnamed x99 -> x167, local copies, waits for them, and re-layouts: 14.8 us -> 53 us
where the time goes in v1:
time: 546 us; the launch traced here: 545 us
  waiting for transfers between devices  223 us (41%)
  other arithmetic  134 us (25%)
  local copies, waits for them, and re-layouts  128 us (23%)
  starting transfers between devices  30.7 us (6%)
  between operations  14.9 us (3%)
  matrix products  14.8 us (3%)
    psum x1, waiting for transfers between devices, per_device(): lax.psum(jnp.concatenate([edge_vec, node_vec]).astype(jnp.bfloat16), 'cut')  136 us
    unnamed x167, local copies, waits for them, and re-layouts  53 us
    all_to_all x2, waiting for transfers between devices, expand_the_racks(): lax.all_to_all(jnp.stack(jnp.split(inp, a_next, 1), 0), axis_name=a_name,...  51 us
    scatter-add x2, other arithmetic, per_device(): grad_table = jnp.zeros((latent, local_width), jnp.float32).at[:, send_col...  47.1 us
    scatter-add x2, other arithmetic, reduce_mirrors(): result = master_part.at[:, mirror_index].add(returned)  45.9 us
    all_to_all x2, waiting for transfers between devices, reduce_mirrors(): lax.all_to_all(mirror_part.astype(jnp.bfloat16), 'cut', split_axis=1, con...  27.5 us
    gather x2, local copies, waits for them, and re-layouts, fetch_mirrors(): outgoing = jnp.take(master_part, mirror_index, axis=1)  24.3 us
    scatter-add x1, other arithmetic, per_device(): jnp.zeros((latent, local_width), jnp.float32).at[:, recv_cols].add(message)  23.3 us
  transfers between devices with their start and end apart: 6, of which 5 were waited for; matrix products, arithmetic and copies ran while one was open for 2% of the time, Pallas kernels for 0%

profile of v1, /device:TPU:2, one launch (start us, length us, event | category | flops | bytes accessed | tf_op | source)
XLA Modules:
  0.0 545.3 jit_solution(9219302339278242080)
XLA Ops:
  7.2 11.5 %all-to-all-start = ((s32[32,1,128]{2,1,0:T(1,128)}), s32[32,1,128]{2,1,0:T(1,128)S(1)}, u32[]{:S(2)}, u32[]{:S(2)}) async-start(s32[32,1,128]{2,1,0:T(1,128)} %bitcast.402), calls=%async_computation | async-start | bytes 32768 | tf_op jit(solution)/shard_map/all_to_all | solution.py:79
  19.4 1.1 copy.38
  20.5 7.9 %all-to-all-done = s32[32,1,128]{2,1,0:T(1,128)S(1)} async-done(((s32[32,1,128]{2,1,0:T(1,128)}), s32[32,1,128]{2,1,0:T(1,128)S(1)}, u32[]{:S(2)}, u32[]{:S(2)}) %all-to-all-start) | async-done | bytes 16416 | tf_op jit(solution)/shard_map/all_to_all | solution.py:79
  28.4 12.1 %gather_fusion = bf16[4096,128]{1,0:T(8,128)(2,1)S(1)} fusion(bf16[128,1024]{0,1:T(8,128)(2,1)S(1)} %copy.38, s32[4096]{0:T(1024)S(1)} %fusion.48), kind=kCustom, calls=%fused_computation.clone | custom fusion | bytes 2113536 | tf_op jit(solution)/shard_map/jit(_take)/gather | solution.py:84
  40.6 2.1 select_bitcast_fusion.3
  62.5 4.1 all-to-all-start.1
  66.7 1.3 copy.36
  68.9 25.3 %all-to-all-done.1 = bf16[32,128,128]{1,2,0:T(8,128)(2,1)S(1)} async-done(((bf16[32,128,128]{1,2,0:T(8,128)(2,1)}), bf16[32,128,128]{1,2,0:T(8,128)(2,1)S(1)}, u32[]{:S(2)}, u32[]{:S(2)}) %all-to-all-start.1) | async-done | bytes 1048608 | tf_op jit(solution)/shard_map/all_to_all | solution.py:12
  94.2 12.1 %gather_fusion.1 = bf16[4096,128]{1,0:T(8,128)(2,1)S(1)} fusion(bf16[128,5120]{0,1:T(8,128)(2,1)S(1)} %pad_maximum_fusion.1, s32[4096]{0:T(1024)S(1)} %get-tuple-element.40), kind=kCustom, calls=%fused_computation.1.clone | custom fusion | bytes 2113536 | tf_op jit(solution)/shard_map/jit(_take)/gather | solution.py:108
  106.4 15.0 %gather_fusion.2 = bf16[4096,128]{1,0:T(8,128)(2,1)} fusion(bf16[128,5120]{0,1:T(8,128)(2,1)S(1)} %pad_maximum_fusion.1, s32[4096]{0:T(1024)S(1)} %get-tuple-element.41), kind=kCustom, calls=%fused_computation.3.clone | custom fusion | bytes 2113536 | tf_op jit(solution)/shard_map/jit(_take)/gather | solution.py:109
  121.4 2.1 select_bitcast_fusion.2
  123.6 2.1 select_bitcast_fusion.1
  125.8 2.3 multiply_convert_fusion
  129.1 0.8 copy-done.1
  130.4 1.8 copy.37
  132.2 23.3 %scatter_custom_fusion = f32[128,5120]{0,1:T(8,128)S(1)} fusion(s32[4096]{0:T(1024)S(1)} %bitcast.400, f32[4096,128]{1,0:T(8,128)} %copy.37, f32[]{:T(128)} %constant.26.clone.1), kind=kCustom, calls=%fused_computation.47 | custom fusion | flops 524288 | bytes 2621952 | tf_op jit(solution)/shard_map/scatter-add | solution.py:118
  155.5 1.1 slice.89
  156.6 5.1 all-to-all-start.2
  161.8 27.5 %all-to-all-done.2 = bf16[128,32,128]{0,2,1:T(8,128)(2,1)} async-done(((bf16[128,32,128]{0,2,1:T(8,128)(2,1)}), bf16[128,32,128]{0,2,1:T(8,128)(2,1)}, u32[]{:S(2)}, u32[]{:S(2)}) %all-to-all-start.2) | async-done | bytes 1048608 | tf_op jit(solution)/shard_map/all_to_all | solution.py:89
  189.3 23.1 %scatter_custom_fusion.1 = f32[128,1024]{0,1:T(8,128)S(1)} fusion(f32[128,1024]{0,1:T(8,128)S(1)} %slice.66, s32[4096]{0:T(1024)S(1)} %bitcast.403, bf16[128,4096]{0,1:T(8,128)(2,1)} %bitcast.103), kind=kCustom, calls=%fused_computation.22 | custom fusion | flops 1048576 | bytes 1572864 | tf_op jit(solution)/shard_map/scatter-add | solution.py:92
  212.6 1.2 multiply_convert_fusion.1
  215.0 1.0 fusion.35
  217.0 12.1 %gather_fusion.3 = bf16[4096,128]{1,0:T(8,128)(2,1)S(1)} fusion(bf16[128,1024]{0,1:T(8,128)(2,1)S(1)} %fusion.25, s32[4096]{0:T(1024)S(1)} %fusion.48), kind=kCustom, calls=%fused_computation.2.clone | custom fusion | bytes 2113536 | tf_op jit(solution)/shard_map/jit(_take)/gather | solution.py:84
  229.1 2.1 select_bitcast_fusion
  251.0 5.0 all-to-all-start.3
  257.1 0.8 fusion.29
  257.9 25.7 %all-to-all-done.3 = bf16[32,128,128]{1,2,0:T(8,128)(2,1)S(1)} async-done(((bf16[32,128,128]{1,2,0:T(8,128)(2,1)}), bf16[32,128,128]{1,2,0:T(8,128)(2,1)S(1)}, u32[]{:S(2)}, u32[]{:S(2)}) %all-to-all-start.3) | async-done | bytes 1048608 | tf_op jit(solution)/shard_map/all_to_all | solution.py:12
  283.8 15.0 %gather_fusion.4 = bf16[4096,128]{1,0:T(8,128)(2,1)} fusion(bf16[128,5120]{0,1:T(8,128)(2,1)S(1)} %pad_maximum_fusion.2, s32[4096]{0:T(1024)S(1)} %copy-done.20), kind=kCustom, calls=%fused_computation.4.clone | custom fusion | bytes 2113536 | tf_op jit(solution)/shard_map/jit(_take)/gather | solution.py:152
  298.8 1.6 copy.40
  300.7 1.7 fusion.12
  304.1 1.2 copy-done.44
  305.3 1.5 fusion.58
  307.1 1.4 fusion.26
  308.5 1.4 fusion.2
  309.9 1.8 fusion.42
  311.7 1.7 fusion.44
  313.4 23.3 %scatter_custom_fusion.2 = f32[128,5120]{0,1:T(8,128)S(1)} fusion(s32[4096]{0:T(1024)} %bitcast.405, f32[4096,128]{1,0:T(8,128)} %fusion.44, f32[]{:T(128)} %constant.26.clone.1), kind=kCustom, calls=%fused_computation.45 | custom fusion | flops 524288 | bytes 2621952 | tf_op jit(solution)/shard_map/scatter-add | solution.py:167
  336.7 23.8 %scatter_fusion = f32[128,5120]{0,1:T(8,128)S(1)} fusion(f32[128,5120]{0,1:T(8,128)S(1)} %scatter_custom_fusion.2, s32[4096]{0:T(1024)S(1)} %bitcast.401, f32[4096,128]{1,0:T(8,128)} %fusion.42), kind=kCustom, calls=%fused_computation.8 | custom fusion | flops 524288 | bytes 6307840 | tf_op jit(solution)/shard_map/scatter-add | solution.py:169
  360.6 1.1 slice.88
  361.7 1.0 reshape.219
  364.6 0.8 dynamic-update-slice.5
  366.2 1.1 dynamic-update-slice.7
  368.4 2.3 copy.44
  371.4 5.0 all-to-all-start.4
  376.4 136.5 %all-reduce.2.cloned.1.call-done = bf16[115456]{0:T(1024)(128)(2,1)} async-done(((bf16[115456]{0:T(1024)(128)(2,1)}), bf16[115456]{0:T(1024)(128)(2,1)}) %all-reduce.2.cloned.1.call-update) | async-done | bytes 230928 | tf_op jit(solution)/shard_map/psum | solution.py:183
  512.8 1.0 convert_element_type.94
  514.7 22.7 %scatter_custom_fusion.4 = f32[128,1024]{0,1:T(8,128)S(1)} fusion(f32[128,1024]{0,1:T(8,128)S(1)} %copy.42, s32[4096]{0:T(1024)} %bitcast.404, bf16[128,4096]{0,1:T(8,128)(2,1)S(1)} %bitcast.390), kind=kCustom, calls=%fused_computation.20 | custom fusion | flops 1048576 | bytes 1572864 | tf_op jit(solution)/shard_map/scatter-add | solution.py:92
  537.4 1.0 copy.43
  (207 shorter events, 53.5 us)
Async XLA Ops:
  7.2 120.9 %copy-start = (bf16[128,128]{1,0:T(8,128)(2,1)S(1)}, bf16[128,128]{1,0:T(8,128)(2,1)}, u32[]{:S(2)}) copy-start(bf16[128,128]{1,0:T(8,128)(2,1)} %param.29) | copy-start | bytes 98308
  7.2 21.2 %all-to-all-start = ((s32[32,1,128]{2,1,0:T(1,128)}), s32[32,1,128]{2,1,0:T(1,128)S(1)}, u32[]{:S(2)}, u32[]{:S(2)}) async-start(s32[32,1,128]{2,1,0:T(1,128)} %bitcast.402), calls=%async_computation | async-start | bytes 32768 | tf_op jit(solution)/shard_map/all_to_all | solution.py:79
  42.7 23.9 %copy-start.39 = (s32[32,2]{0,1:T(2,128)S(1)}, s32[32,2]{0,1:T(2,128)}, u32[]{:S(2)}) copy-start(s32[32,2]{0,1:T(2,128)} %param.24) | copy-start | bytes 772
  42.7 24.0 %copy-start.10 = (bf16[128,4096]{1,0:T(8,128)(2,1)S(1)}, bf16[128,4096]{1,0:T(8,128)(2,1)}, u32[]{:S(2)}) copy-start(bf16[128,4096]{1,0:T(8,128)(2,1)} %param.22) | copy-start | bytes 3145732
  62.5 5.5 %copy-start.30 = (s32[32,2,128]{2,1,0:T(2,128)S(1)}, s32[32,2,128]{2,1,0:T(2,128)}, u32[]{:S(2)}) copy-start(s32[32,2,128]{2,1,0:T(2,128)} %param.25) | copy-start | bytes 98308
  62.5 31.6 %all-to-all-start.1 = ((bf16[32,128,128]{1,2,0:T(8,128)(2,1)}), bf16[32,128,128]{1,2,0:T(8,128)(2,1)S(1)}, u32[]{:S(2)}, u32[]{:S(2)}) async-start(bf16[32,128,128]{1,2,0:T(8,128)(2,1)} %constant_dynamic-update-slice_fusion), calls=%async_computation.1 | async-start | bytes 2097152 | tf_op jit(solution)/shard_map/all_to_all | solution.py:12
  68.2 55.4 %copy-start.27 = (pred[4096]{0:T(1024)(128)(4,1)}, pred[4096]{0:T(1024)(128)(4,1)S(1)}, u32[]{:S(2)}) copy-start(pred[4096]{0:T(1024)(128)(4,1)S(1)} %compare_and_fusion) | copy-start | bytes 12292
  68.2 38.2 %copy-start.19 = (s32[4096]{0:T(1024)}, s32[4096]{0:T(1024)S(1)}, u32[]{:S(2)}) copy-start(s32[4096]{0:T(1024)S(1)} %get-tuple-element.41) | copy-start | bytes 49156
  68.8 63.4 %copy-start.23 = (s32[4096,1]{0,1:T(1,128)}, s32[4096,1]{0,1:T(1,128)S(1)}, u32[]{:S(2)}) copy-start(s32[4096,1]{0,1:T(1,128)S(1)} %get-tuple-element.26) | copy-start | bytes 49156
  121.4 2.2 copy-start.5
  121.4 4.4 copy-start.11
  121.4 4.4 copy-start.21
  121.4 4.4 copy-start.42
  123.6 4.5 copy-start.13
  125.8 2.3 copy-start.15
  128.1 1.8 copy-start.32
  128.1 1.8 copy-start.40
  128.6 1.3 copy-start.1
  156.6 32.7 %all-to-all-start.2 = ((bf16[128,32,128]{0,2,1:T(8,128)(2,1)}), bf16[128,32,128]{0,2,1:T(8,128)(2,1)}, u32[]{:S(2)}, u32[]{:S(2)}) async-start(bf16[128,32,128]{0,2,1:T(8,128)(2,1)} %bitcast.392), calls=%async_computation.2 | async-start | bytes 2097152 | tf_op jit(solution)/shard_map/all_to_all | solution.py:89
  161.7 50.8 %copy-start.43 = (f32[128]{0:T(128)S(1)}, f32[128]{0:T(128)}, u32[]{:S(2)}) copy-start(f32[128]{0:T(128)} %param.33) | copy-start | bytes 1540
  161.8 52.0 %copy-start.31 = (s32[4096,1]{0,1:T(1,128)}, s32[4096,1]{0,1:T(1,128)S(1)}, u32[]{:S(2)}) copy-start(s32[4096,1]{0,1:T(1,128)S(1)} %compare_select_fusion.1) | copy-start | bytes 49156
  212.5 1.3 copy-start.29
  212.5 1.6 copy-start.6
  212.5 1.6 copy-start.34
  212.6 2.4 copy-start.17
  212.6 2.4 copy-start.41
  214.9 1.8 copy-start.25
  216.8 40.0 %copy-start.8 = (bf16[128,1024]{0,1:T(8,128)(2,1)}, bf16[128,1024]{0,1:T(8,128)(2,1)S(1)}, u32[]{:S(2)}) copy-start(bf16[128,1024]{0,1:T(8,128)(2,1)S(1)} %get-tuple-element.39) | copy-start | bytes 786436
  251.0 32.6 %all-to-all-start.3 = ((bf16[32,128,128]{1,2,0:T(8,128)(2,1)}), bf16[32,128,128]{1,2,0:T(8,128)(2,1)S(1)}, u32[]{:S(2)}, u32[]{:S(2)}) async-start(bf16[32,128,128]{1,2,0:T(8,128)(2,1)} %constant_dynamic-update-slice_fusion.32), calls=%async_computation.3 | async-start | bytes 2097152 | tf_op jit(solution)/shard_map/all_to_all | solution.py:12
  256.0 256.8 %all-reduce.2.cloned.1.call-start = ((), (), s32[]{:S(2)}) async-start(), calls=%async_computation.5 | async-start | bytes 462848 | tf_op jit(solution)/shard_map/psum | solution.py:183
  256.7 27.0 %copy-start.20 = (s32[4096]{0:T(1024)S(1)}, s32[4096]{0:T(1024)}, u32[]{:S(2)}) copy-start(s32[4096]{0:T(1024)} %copy-done.19) | copy-start | bytes 49156
  283.7 16.7 %copy-start.28 = (pred[4096]{0:T(1024)(128)(4,1)S(1)}, pred[4096]{0:T(1024)(128)(4,1)}, u32[]{:S(2)}) copy-start(pred[4096]{0:T(1024)(128)(4,1)} %copy-done.27) | copy-start | bytes 12292
  283.8 16.7 %copy-start.33 = (f32[128]{0:T(128)S(1)}, f32[128]{0:T(128)}, u32[]{:S(2)}) copy-start(f32[128]{0:T(128)} %param.30) | copy-start | bytes 1540
  298.8 1.9 copy-start.2
  303.7 1.6 copy-start.44
  305.3 1.5 copy-start.12
  305.3 1.5 copy-start.14
  305.3 1.9 copy-start.16
  307.1 1.4 copy-start.22
  313.4 23.3 %copy-start.24 = (s32[4096,1]{0,1:T(1,128)S(1)}, s32[4096,1]{0,1:T(1,128)}, u32[]{:S(2)}) copy-start(s32[4096,1]{0,1:T(1,128)} %copy-done.23) | copy-start | bytes 49156
  360.5 3.5 copy-start.38
  360.6 3.8 copy-start.37
  360.6 6.7 %copy-start.35 = (bf16[128]{0:T(256)(128)(2,1)S(1)}, bf16[128]{0:T(256)(128)(2,1)}, u32[]{:S(2)}) copy-start(bf16[128]{0:T(256)(128)(2,1)} %get-tuple-element.18) | copy-start | bytes 772
  360.6 6.9 %copy-start.36 = (bf16[128]{0:T(256)(128)(2,1)S(1)}, bf16[128]{0:T(256)(128)(2,1)}, u32[]{:S(2)}) copy-start(bf16[128]{0:T(256)(128)(2,1)} %reduce.4) | copy-start | bytes 772
  361.7 9.2 %copy-start.7 = (bf16[128,1024]{1,0:T(8,128)(2,1)S(1)}, bf16[128,1024]{1,0:T(8,128)(2,1)}, u32[]{:S(2)}) copy-start(bf16[128,1024]{1,0:T(8,128)(2,1)} %param.37) | copy-start | bytes 786436
  361.7 9.2 %copy-start.9 = (bf16[128,1024]{0,1:T(8,128)(2,1)S(1)}, bf16[128,1024]{0,1:T(8,128)(2,1)}, u32[]{:S(2)}) copy-start(bf16[128,1024]{0,1:T(8,128)(2,1)} %copy-done.8) | copy-start | bytes 786436
  361.7 9.2 %copy-start.26 = (bf16[128,256]{1,0:T(8,128)(2,1)S(1)}, bf16[128,256]{1,0:T(8,128)(2,1)}, u32[]{:S(2)}) copy-start(bf16[128,256]{1,0:T(8,128)(2,1)} %param.32) | copy-start | bytes 196612
  371.4 143.3 %all-to-all-start.4 = ((bf16[128,32,128]{0,2,1:T(8,128)(2,1)}), bf16[128,32,128]{0,2,1:T(8,128)(2,1)S(1)}, u32[]{:S(2)}, u32[]{:S(2)}) async-start(bf16[128,32,128]{0,2,1:T(8,128)(2,1)} %bitcast.96), calls=%async_computation.4 | async-start | bytes 2097152 | tf_op jit(solution)/shard_map/all_to_all | solution.py:89
  (3 other events, 2.9 us)
Sparse Core Ops, SparseCore 0:
  368.5 144.2 all-reduce.1
